TPU v7x, 128 devices: a whole 4x4x4 slice. The times are simulated.
128 devices in a mesh: dp: 4 (over x), ctx: 32 (over z, y, core).
Axes of the slice: x: 4, y: 4, z: 4, core: 2. Of those that a mesh axis runs over, the one named last changes fastest.
Arguments:
- queries: bfloat16 [4, 8192, 2048], P('dp', 'ctx'), may hold values from -6 to 6
- keys: bfloat16 [4, 8192, 2048], P('dp', 'ctx'), may hold values from -6 to 6
- values: bfloat16 [4, 8192, 2048], P('dp', 'ctx'), may hold values from -6 to 6
- gain: float32 [2048], replicated, may hold values from 0.1 to 1.9
- out_weight: bfloat16 [2048, 4096], P('dp'), may hold values from -0.125 to 0.125
- grad_out: bfloat16 [4, 8192, 4096], P('dp', 'ctx'), may hold values from -6 to 6
Outputs:
- layer_out: bfloat16 [4, 8192, 4096], P('dp', 'ctx')
- grad_queries: bfloat16 [4, 8192, 2048], P('dp', 'ctx')
- grad_keys: bfloat16 [4, 8192, 2048], P('dp', 'ctx')
- grad_values: bfloat16 [4, 8192, 2048], P('dp', 'ctx')
- grad_weight: float32 [2048, 4096], P(('dp', 'ctx'))
All inputs are finite; a program needn't handle non-finite values.
Results may differ from a plain program's by a relative error of at most 0.015.
Values may be sent and summed in bfloat16 or wider, within the bound.
No kernel may reach another device: no remote copies, remote signals or barrier semaphores. Data moves between devices by JAX's collectives and lax.ppermute only.
A program may use at most 192 MiB of HBM per device.

v0:
```python
import math
import jax
import jax.numpy as jnp
from jax import lax
from jax.sharding import PartitionSpec as P

HD = 128
EPSILON = 1e-06
HIGHEST = lax.Precision.HIGHEST


def prefix(part, axis, combine, identity, reverse):
    count = lax.axis_size(axis)
    place = lax.axis_index(axis)
    ahead = count - 1 - place if reverse else place
    gathered = lax.all_gather(part, axis)
    state = jnp.zeros_like(part) + jnp.asarray(identity, part.dtype)

    def one(turn, state):
        source = count - 1 - turn if reverse else turn
        return combine(state, lax.dynamic_index_in_dim(gathered, source, 0, False))

    return lax.fori_loop(0, ahead, one, state)


def add_terms(earlier, later_part):
    return earlier + later_part


def shards(queries, keys, values, gain, out_weight, grad_out):
    tok_rows = queries.shape[1]
    feat_width = queries.shape[2]
    head_count = feat_width // HD
    model_width = grad_out.shape[2]
    query_rows = queries.reshape(tok_rows, head_count, HD)
    key_rows = keys.reshape(tok_rows, head_count, HD)
    value_rows = values.reshape(tok_rows, head_count, HD)
    causal = lax.broadcasted_iota(jnp.int32, (tok_rows, tok_rows), 0) >= lax.broadcasted_iota(
        jnp.int32, (tok_rows, tok_rows), 1
    )
    scores = jnp.einsum("thd,shd->hts", query_rows, key_rows, preferred_element_type=jnp.float32)
    weights = jnp.where(causal, scores, 0.0).astype(jnp.bfloat16)
    local_out = jnp.einsum("hts,shd->thd", weights, value_rows, preferred_element_type=jnp.float32)
    local_state = jnp.einsum(
        "shd,she->hde", key_rows, value_rows, preferred_element_type=jnp.float32
    )
    carried = prefix(local_state, "ctx", add_terms, jnp.zeros_like(local_state), False)
    state_out = jnp.einsum(
        "thd,hde->the", query_rows.astype(jnp.float32), carried, precision=HIGHEST
    )
    attended = local_out + state_out
    inv_rms = lax.rsqrt(jnp.mean(attended * attended, axis=-1, keepdims=True) + EPSILON)
    unit_out = attended * inv_rms
    gain_heads = gain.reshape(head_count, HD)
    normed = (unit_out * gain_heads).astype(jnp.bfloat16).reshape(tok_rows, feat_width)
    grad_rows = grad_out.reshape(tok_rows, model_width)
    full_weight = lax.all_gather(out_weight, "dp", axis=0, tiled=True)
    layer_rows = jnp.dot(normed, full_weight, preferred_element_type=jnp.float32)
    layer_out = layer_rows.astype(jnp.bfloat16).reshape(1, tok_rows, model_width)
    shared_cols = lax.all_to_all(normed, "dp", split_axis=1, concat_axis=0, tiled=True)
    grad_normed = lax.dot_general(
        grad_rows, full_weight, (((1,), (1,)), ((), ())), preferred_element_type=jnp.float32
    )
    weight_term = lax.dot_general(
        shared_cols,
        lax.all_gather(grad_rows, "dp", axis=0, tiled=True),
        (((0,), (0,)), ((), ())),
        preferred_element_type=jnp.float32,
    )
    token_count = lax.axis_size("dp") * lax.axis_size("ctx") * tok_rows
    grad_weight = lax.psum_scatter(
        weight_term.astype(jnp.bfloat16), "ctx", scatter_dimension=0, tiled=True
    ).astype(jnp.float32) * (1.0 / math.sqrt(token_count))
    grad_unit = grad_normed.reshape(tok_rows, head_count, HD) * gain_heads
    grad_attn = inv_rms * (
        grad_unit - unit_out * jnp.mean(grad_unit * unit_out, axis=-1, keepdims=True)
    )
    grad_attn = grad_attn.astype(jnp.bfloat16)
    grad_scores = jnp.einsum(
        "the,she->hts", grad_attn, value_rows, preferred_element_type=jnp.float32
    )
    grad_scores = jnp.where(causal, grad_scores, 0.0).astype(jnp.bfloat16)
    local_grad = jnp.einsum(
        "thd,the->hde", query_rows, grad_attn, preferred_element_type=jnp.float32
    )
    later = prefix(local_grad, "ctx", add_terms, jnp.zeros_like(local_grad), True)
    grad_query = jnp.einsum(
        "hts,shd->thd", grad_scores, key_rows, preferred_element_type=jnp.float32
    )
    grad_query = grad_query + jnp.einsum(
        "the,hde->thd", grad_attn.astype(jnp.float32), carried, precision=HIGHEST
    )
    grad_key = jnp.einsum(
        "hts,thd->shd", grad_scores, query_rows, preferred_element_type=jnp.float32
    )
    grad_key = grad_key + jnp.einsum(
        "she,hde->shd", value_rows.astype(jnp.float32), later, precision=HIGHEST
    )
    grad_value = jnp.einsum("hts,the->she", weights, grad_attn, preferred_element_type=jnp.float32)
    grad_value = grad_value + jnp.einsum(
        "shd,hde->she", key_rows.astype(jnp.float32), later, precision=HIGHEST
    )
    out_shape = (1, tok_rows, feat_width)
    return (
        layer_out,
        grad_query.astype(jnp.bfloat16).reshape(out_shape),
        grad_key.astype(jnp.bfloat16).reshape(out_shape),
        grad_value.astype(jnp.bfloat16).reshape(out_shape),
        grad_weight,
    )


def solution(mesh):
    in_specs = (
        P("dp", "ctx", None),
        P("dp", "ctx", None),
        P("dp", "ctx", None),
        P(),
        P("dp", None),
        P("dp", "ctx", None),
    )
    out_specs = (
        P("dp", "ctx", None),
        P("dp", "ctx", None),
        P("dp", "ctx", None),
        P("dp", "ctx", None),
        P(("dp", "ctx"), None),
    )
    return jax.shard_map(shards, mesh=mesh, in_specs=in_specs, out_specs=out_specs, check_vma=False)
```

profile of v0, /device:TPU:0, one launch (start us, length us, event | category | flops | bytes accessed | tf_op | source)
XLA Modules:
  0.0 650.7 jit_solution(872384761315528733)
XLA Ops:
  7.2 1.5 copy.78
  16.6 2.2 fusion.12
  18.7 109.2 %all-gather.10.cloned.1.call-done = f32[512,128,128]{2,1,0:T(8,128)} async-done(((f32[16,128,128]{2,1,0:T(8,128)}), f32[512,128,128]{2,1,0:T(8,128)}) %all-gather.10.cloned.1.call-update) | async-done | bytes 33554448 | tf_op jit(solution)/shard_map/all_gather | solution.py:16
  128.1 4.1 multiply_reduce_fusion.1
  132.2 150.6 %all-gather.8.cloned.1.call-done = bf16[2048,4096]{1,0:T(8,128)(2,1)} async-done(((bf16[512,4096]{1,0:T(8,128)(2,1)}), bf16[2048,4096]{1,0:T(8,128)(2,1)}) %all-gather.8.cloned.1.call-update) | async-done | bytes 16777232 | tf_op jit(solution)/shard_map/all_gather | solution.py:57
  282.8 12.6 %multiply_reduce_fusion = (f32[256,16]{0,1:T(8,128)S(1)}, f32[256,16,128]{0,2,1:T(8,128)S(1)}) fusion(f32[256,16,128]{0,2,1:T(8,128)} %get-tuple-element.128, f32[16,128]{1,0:T(8,128)S(1)} %bitcast.102, f32[256,16]{0,1:T(8,128)S(1)} %add_rsqrt_fusion, bf16[16,128,4096]{2,1,0:T(8,128)(2,1)} %bitcast.80, bf16[1,256,4096]{2,1,0:T(8,128)(2,1)} %param.15), kind=kOutput, calls=%fused_computation.18 | convolution fusion | flops 4297060352 | bytes 23109632 | tf_op jit(solution)/shard_map/dot_general | solution.py:61
  295.5 1.7 multiply_convert_fusion
  297.1 2.3 copy.69
  299.5 4.2 all-to-all-start
  303.9 75.8 %all-gather.14.cloned.1.call-done = bf16[1,1024,4096]{2,1,0:T(8,128)(2,1)} async-done(((bf16[1,256,4096]{2,1,0:T(8,128)(2,1)}), bf16[1,1024,4096]{2,1,0:T(8,128)(2,1)}) %all-gather.14.cloned.1.call-update) | async-done | bytes 8388624 | tf_op jit(solution)/shard_map/all_gather | solution.py:66
  379.8 10.2 %fusion.2 = bf16[512,4096]{1,0:T(8,128)(2,1)} fusion(bf16[1024,512]{1,0:T(8,128)(2,1)} %bitcast.23, bf16[1,1024,4096]{2,1,0:T(8,128)(2,1)} %all-gather.14.cloned.1.call-done), kind=kOutput, calls=%fused_computation.4 | convolution fusion | flops 4297064448 | bytes 13631488 | tf_op jit(solution)/shard_map/dot_general | solution.py:64
  390.1 2.7 convolution_bitcast_fusion
  392.7 2.6 copy.65
  397.9 2.1 fusion.7
  400.0 2.3 copy.70
  402.3 3.5 fusion.24
  405.8 11.9 %fusion.5 = bf16[1,256,4096]{2,1,0:T(8,128)(2,1)} fusion(bf16[256,2048]{0,1:T(8,128)(2,1)S(1)} %bitcast.90, bf16[2048,4096]{1,0:T(8,128)(2,1)} %all-gather.8.cloned.1.call-done), kind=kOutput, calls=%fused_computation.6 | convolution fusion | flops 4296015872 | bytes 19922944 | tf_op jit(solution)/shard_map/dot_general | solution.py:58
  417.8 56.0 %reduce-scatter.2.cloned.1.call-done = bf16[16,4096]{1,0:T(8,128)(2,1)} async-done(((bf16[512,4096]{1,0:T(8,128)(2,1)}), bf16[16,4096]{1,0:T(8,128)(2,1)}) %reduce-scatter.2.cloned.1.call-update) | async-done | bytes 131088 | tf_op jit(solution)/shard_map/reduce_scatter | solution.py:71
  473.7 1.6 convert_multiply_fusion
  475.3 113.5 %all-gather.12.cloned.1.call-done = f32[512,128,128]{2,1,0:T(8,128)} async-done(((f32[16,128,128]{2,1,0:T(8,128)}), f32[512,128,128]{2,1,0:T(8,128)}) %all-gather.12.cloned.1.call-update) | async-done | bytes 33554448 | tf_op jit(solution)/shard_map/all_gather | solution.py:16
  589.0 47.1 %while.23 = (s32[]{:T(128)}, f32[16,128,128]{2,1,0:T(8,128)S(1)}, s32[]{:T(128)}, f32[32,16,128,128]{3,2,1,0:T(8,128)}, s32[]{:T(128)}, /*index=5*/s32[]{:T(128)}, s32[]{:T(128)}, s32[]{:T(128)}) while((s32[]{:T(128)}, f32[16,128,128]{2,1,0:T(8,128)S(1)}, s32[]{:T(128)}, f32[32,16,128,128]{3,2,1,0:T(8,128)}, s32[]{:T(128)}, ...), condition=%wide.region_5.6_spmd, body=%wide.region_4.5_spmd.sunk | while | flops 262150 | bytes 3145871 | solution.py:23
  598.1 1.5 bitcast_add_fusion.8
  626.8 1.5 bitcast_add_fusion.8
  640.0 2.7 add_convert_fusion
  (85 shorter events, 59.3 us)
Async XLA Ops:
  7.2 120.8 %all-gather.10.cloned.1.call-start = ((), (), s32[]{:S(2)}) async-start(), calls=%async_computation.4 | async-start | bytes 34603008 | tf_op jit(solution)/shard_map/all_gather | solution.py:16
  7.2 2.5 copy-start.12
  8.8 1.0 copy-start.5
  9.7 1.7 copy-start.3
  11.4 271.4 %all-gather.8.cloned.1.call-start = ((), (), s32[]{:S(2)}) async-start(), calls=%async_computation.2 | async-start | bytes 20971520 | tf_op jit(solution)/shard_map/all_gather | solution.py:57
  12.2 2.3 copy-start.6
  12.2 367.6 %all-gather.14.cloned.1.call-start = ((), (), s32[]{:S(2)}) async-start(), calls=%async_computation.6 | async-start | bytes 10485760 | tf_op jit(solution)/shard_map/all_gather | solution.py:66
  14.4 113.6 %copy-start = (bf16[32,8,16,128]{3,2,1,0:T(8,128)(2,1)}, bf16[32,8,16,128]{3,2,1,0:T(8,128)(2,1)S(1)}, u32[]{:S(2)}) copy-start(bf16[32,8,16,128]{3,2,1,0:T(8,128)(2,1)S(1)} %copy.77) | copy-start | bytes 3145732
  15.2 1.3 copy-start.11
  128.0 154.8 %copy-start.13 = (f32[2048]{0:T(1024)S(1)}, f32[2048]{0:T(1024)}, u32[]{:S(2)}) copy-start(f32[2048]{0:T(1024)} %param.13) | copy-start | bytes 24580
  282.8 12.6 %copy-start.10 = (f32[256,16,128]{0,2,1:T(8,128)S(1)}, f32[256,16,128]{0,2,1:T(8,128)}, u32[]{:S(2)}) copy-start(f32[256,16,128]{0,2,1:T(8,128)} %get-tuple-element.128) | copy-start | bytes 6291460
  299.5 80.3 %all-to-all-start = ((bf16[256,4,512]{2,0,1:T(8,128)(2,1)}), bf16[256,4,512]{2,0,1:T(8,128)(2,1)}, u32[]{:S(2)}, u32[]{:S(2)}) async-start(bf16[256,4,512]{2,0,1:T(8,128)(2,1)} %copy.69), calls=%async_computation | async-start | bytes 2097152 | tf_op jit(solution)/shard_map/all_to_all | solution.py:60
  303.7 170.0 %reduce-scatter.2.cloned.1.call-start = ((), (), s32[]{:S(2)}) async-start(), calls=%async_computation.3 | async-start | bytes 4325376 | tf_op jit(solution)/shard_map/reduce_scatter | solution.py:71
  390.0 198.9 %all-gather.12.cloned.1.call-start = ((), (), s32[]{:S(2)}) async-start(), calls=%async_computation.5 | async-start | bytes 34603008 | tf_op jit(solution)/shard_map/all_gather | solution.py:16
  395.3 1.2 copy-start.4
  396.6 1.4 copy-start.8
  402.3 3.5 copy-start.2
  636.1 1.2 copy-start.1
  636.1 1.9 copy-start.9
  638.6 1.4 copy-start.7
Sparse Core Ops, SparseCore 0:
  11.6 116.3 all-gather.9
  129.6 153.2 all-gather.7
  284.5 95.2 all-gather.13
  390.1 83.5 reduce-scatter.1
  475.8 113.0 all-gather.11
where the time goes:
time: 652 us; the launch traced here: 651 us
  waiting for transfers between devices  507 us (78%)
  matrix products  57.5 us (9%)
  other arithmetic  49.5 us (8%)
  local copies, waits for them, and re-layouts  17.5 us (3%)
  between operations  14 us (2%)
    all_gather x2, waiting for transfers between devices, prefix(): gathered = lax.all_gather(part, axis)  223 us
    all_gather x1, waiting for transfers between devices, shards(): full_weight = lax.all_gather(out_weight, 'dp', axis=0, tiled=True)  151 us
    all_gather x1, waiting for transfers between devices, shards(): lax.all_gather(grad_rows, 'dp', axis=0, tiled=True)  75.8 us
    reduce_scatter x1, waiting for transfers between devices, shards(): lax.psum_scatter(weight_term.astype(jnp.bfloat16), 'ctx', scatter_dimensi...  56 us
    add x31, other arithmetic, add_terms(): return earlier + later_part  46.1 us
  transfers between devices with their start and end apart: 6, of which 5 were waited for; matrix products, arithmetic and copies ran while one was open for 8% of the time, Pallas kernels for 0%

commit v1 on v0

--- a/solution.py
+++ b/solution.py
@@ -54,7 +54,8 @@
     gain_heads = gain.reshape(head_count, HD)
     normed = (unit_out * gain_heads).astype(jnp.bfloat16).reshape(tok_rows, feat_width)
     grad_rows = grad_out.reshape(tok_rows, model_width)
-    full_weight = lax.all_gather(out_weight, "dp", axis=0, tiled=True)
+    outgoing = jnp.stack([out_weight] * lax.axis_size("dp"))
+    full_weight = jnp.concatenate(lax.all_to_all(outgoing, "dp", 0, 0), axis=0)
     layer_rows = jnp.dot(normed, full_weight, preferred_element_type=jnp.float32)
     layer_out = layer_rows.astype(jnp.bfloat16).reshape(1, tok_rows, model_width)
     shared_cols = lax.all_to_all(normed, "dp", split_axis=1, concat_axis=0, tiled=True)

time: 652 us -> 584 us (0.90)
  waiting for transfers between devices: 507 us -> 423 us
  local copies, waits for them, and re-layouts: 17.5 us -> 24.9 us
  starting transfers between devices: 4.62 us -> 11.7 us
    all_gather x1 -> x0, waiting for transfers between devices: 151 us -> none  [shards(): full_weight = lax.all_gather(out_weight, 'dp', axis=0, tiled=True)]
    all_to_all x0 -> x1, waiting for transfers between devices: none -> 144 us  [shards(): full_weight = jnp.concatenate(lax.all_to_all(outgoing, 'dp', 0, 0), axis=0)]
    all_gather x1, waiting for transfers between devices: 75.8 us -> 0.02 us  [shards(): lax.all_gather(grad_rows, 'dp', axis=0, tiled=True)]
    all_gather x2, waiting for transfers between devices: 223 us -> 209 us  [prefix(): gathered = lax.all_gather(part, axis)]
    all_to_all x1, waiting for transfers between devices: 0.01 us -> 11.3 us  [shards(): lax.all_to_all(normed, 'dp', split_axis=1, concat_axis=0, tiled=True)]
    another operation x2 -> x3, local copies, waits for them, and re-layouts: 0.19 us -> 7.65 us  [the longest x1 7.46 us: shards(): outgoing = jnp.stack([out_weight] * lax.axis_size('dp'))]
    all_to_all x0 -> x1, starting transfers between devices: none -> 7.11 us  [shards(): full_weight = jnp.concatenate(lax.all_to_all(outgoing, 'dp', 0, 0), axis=0)]
  transfers between devices with their start and end apart: 6 -> 6, of which waited for: 5 -> 5; matrix products, arithmetic and copies ran while one was open for 8% -> 10% of each run, Pallas kernels for 0% -> 0%
where the time goes in v1:
time: 584 us; the launch traced here: 582 us
  waiting for transfers between devices  423 us (72%)
  matrix products  57.6 us (10%)
  other arithmetic  49.5 us (8%)
  local copies, waits for them, and re-layouts  24.9 us (4%)
  between operations  14 us (2%)
  starting transfers between devices  11.7 us (2%)
    all_gather x2, waiting for transfers between devices, prefix(): gathered = lax.all_gather(part, axis)  209 us
    all_to_all x1, waiting for transfers between devices, shards(): full_weight = jnp.concatenate(lax.all_to_all(outgoing, 'dp', 0, 0), axis=0)  144 us
    reduce_scatter x1, waiting for transfers between devices, shards(): lax.psum_scatter(weight_term.astype(jnp.bfloat16), 'ctx', scatter_dimensi...  58.2 us
    add x31, other arithmetic, add_terms(): return earlier + later_part  46.1 us
    dot_general x1, matrix products, shards(): lax.dot_general(grad_rows, full_weight, (((1,), (1,)), ((), ())), preferr...  12.6 us
    dot_general x1, matrix products, shards(): jnp.dot(normed, full_weight, preferred_element_type=jnp.float32)  12 us
  transfers between devices with their start and end apart: 6, of which 5 were waited for; matrix products, arithmetic and copies ran while one was open for 10% of the time, Pallas kernels for 0%

profile of v1, /device:TPU:0, one launch (start us, length us, event | category | flops | bytes accessed | tf_op | source)
XLA Modules:
  0.0 582.1 jit_solution(593718523930405532)
XLA Ops:
  7.2 1.5 copy.78
  11.5 7.5 %stack.2 = bf16[4,512,4096]{2,1,0:T(8,128)(2,1)} broadcast(bf16[512,4096]{1,0:T(8,128)(2,1)} %param.14), dimensions={1,2} | broadcast | bytes 20971520 | tf_op jit(solution)/shard_map/stack | solution.py:57
  19.0 7.1 %all-to-all-start = ((bf16[4,512,4096]{2,1,0:T(8,128)(2,1)}), bf16[4,512,4096]{2,1,0:T(8,128)(2,1)}, u32[]{:S(2)}, u32[]{:S(2)}) async-start(bf16[4,512,4096]{2,1,0:T(8,128)(2,1)} %stack.2), calls=%async_computation | async-start | bytes 33554432 | tf_op jit(solution)/shard_map/all_to_all | solution.py:58
  30.4 2.2 fusion.12
  32.6 95.4 %all-gather.7.cloned.1.call-done = f32[512,128,128]{2,1,0:T(8,128)} async-done(((f32[16,128,128]{2,1,0:T(8,128)}), f32[512,128,128]{2,1,0:T(8,128)}) %all-gather.7.cloned.1.call-update) | async-done | bytes 33554448 | tf_op jit(solution)/shard_map/all_gather | solution.py:16
  128.1 4.1 multiply_reduce_fusion.1
  132.2 144.1 %all-to-all-done = bf16[4,512,4096]{2,1,0:T(8,128)(2,1)} async-done(((bf16[4,512,4096]{2,1,0:T(8,128)(2,1)}), bf16[4,512,4096]{2,1,0:T(8,128)(2,1)}, u32[]{:S(2)}, u32[]{:S(2)}) %all-to-all-start) | async-done | bytes 16777248 | tf_op jit(solution)/shard_map/all_to_all | solution.py:58
  276.4 12.6 %multiply_reduce_fusion = (f32[256,16]{0,1:T(8,128)S(1)}, f32[256,16,128]{0,2,1:T(8,128)S(1)}) fusion(f32[256,16,128]{0,2,1:T(8,128)} %get-tuple-element.128, f32[16,128]{1,0:T(8,128)S(1)} %bitcast.102, f32[256,16]{0,1:T(8,128)S(1)} %add_rsqrt_fusion, bf16[16,128,4096]{2,1,0:T(8,128)(2,1)} %bitcast.11, bf16[1,256,4096]{2,1,0:T(8,128)(2,1)} %param.15), kind=kOutput, calls=%fused_computation.18 | convolution fusion | flops 4297060352 | bytes 23109632 | tf_op jit(solution)/shard_map/dot_general | solution.py:62
  289.0 1.7 multiply_convert_fusion
  290.7 2.3 copy.69
  293.0 4.2 all-to-all-start.1
  297.5 11.3 %all-to-all-done.1 = bf16[256,4,512]{2,0,1:T(8,128)(2,1)} async-done(((bf16[256,4,512]{2,0,1:T(8,128)(2,1)}), bf16[256,4,512]{2,0,1:T(8,128)(2,1)}, u32[]{:S(2)}, u32[]{:S(2)}) %all-to-all-start.1) | async-done | bytes 1048608 | tf_op jit(solution)/shard_map/all_to_all | solution.py:61
  308.8 10.4 %fusion.2 = bf16[512,4096]{1,0:T(8,128)(2,1)} fusion(bf16[1024,512]{1,0:T(8,128)(2,1)} %bitcast.24, bf16[1,1024,4096]{2,1,0:T(8,128)(2,1)} %all-gather.11.cloned.1.call-done), kind=kOutput, calls=%fused_computation.4 | convolution fusion | flops 4297064448 | bytes 13631488 | tf_op jit(solution)/shard_map/dot_general | solution.py:65
  319.2 2.7 convolution_bitcast_fusion
  321.9 2.5 copy.65
  327.0 2.1 fusion.7
  329.1 2.3 copy.70
  331.4 3.5 fusion.24
  334.9 12.0 %fusion.5 = bf16[1,256,4096]{2,1,0:T(8,128)(2,1)} fusion(bf16[256,2048]{0,1:T(8,128)(2,1)S(1)} %bitcast.90, bf16[2048,4096]{1,0:T(8,128)(2,1)} %bitcast.7), kind=kOutput, calls=%fused_computation.6 | convolution fusion | flops 4296015872 | bytes 19922944 | tf_op jit(solution)/shard_map/dot_general | solution.py:59
  346.9 58.2 %reduce-scatter.2.cloned.1.call-done = bf16[16,4096]{1,0:T(8,128)(2,1)} async-done(((bf16[512,4096]{1,0:T(8,128)(2,1)}), bf16[16,4096]{1,0:T(8,128)(2,1)}) %reduce-scatter.2.cloned.1.call-update) | async-done | bytes 131088 | tf_op jit(solution)/shard_map/reduce_scatter | solution.py:72
  405.1 1.6 convert_multiply_fusion
  406.7 113.6 %all-gather.9.cloned.1.call-done = f32[512,128,128]{2,1,0:T(8,128)} async-done(((f32[16,128,128]{2,1,0:T(8,128)}), f32[512,128,128]{2,1,0:T(8,128)}) %all-gather.9.cloned.1.call-update) | async-done | bytes 33554448 | tf_op jit(solution)/shard_map/all_gather | solution.py:16
  520.4 47.1 %while.23 = (s32[]{:T(128)}, f32[16,128,128]{2,1,0:T(8,128)S(1)}, s32[]{:T(128)}, f32[32,16,128,128]{3,2,1,0:T(8,128)}, s32[]{:T(128)}, /*index=5*/s32[]{:T(128)}, s32[]{:T(128)}, s32[]{:T(128)}) while((s32[]{:T(128)}, f32[16,128,128]{2,1,0:T(8,128)S(1)}, s32[]{:T(128)}, f32[32,16,128,128]{3,2,1,0:T(8,128)}, s32[]{:T(128)}, ...), condition=%wide.region_5.6_spmd, body=%wide.region_4.5_spmd.sunk | while | flops 262150 | bytes 3145871 | solution.py:23
  571.4 2.7 add_convert_fusion
  (85 shorter events, 61.6 us)
Async XLA Ops:
  7.2 120.8 %all-gather.7.cloned.1.call-start = ((), (), s32[]{:S(2)}) async-start(), calls=%async_computation.4 | async-start | bytes 34603008 | tf_op jit(solution)/shard_map/all_gather | solution.py:16
  7.2 2.6 copy-start.12
  8.8 1.0 copy-start.5
  9.8 1.7 copy-start.3
  19.0 257.4 %all-to-all-start = ((bf16[4,512,4096]{2,1,0:T(8,128)(2,1)}), bf16[4,512,4096]{2,1,0:T(8,128)(2,1)}, u32[]{:S(2)}, u32[]{:S(2)}) async-start(bf16[4,512,4096]{2,1,0:T(8,128)(2,1)} %stack.2), calls=%async_computation | async-start | bytes 33554432 | tf_op jit(solution)/shard_map/all_to_all | solution.py:58
  26.1 2.3 copy-start.6
  26.1 271.4 %all-gather.11.cloned.1.call-start = ((), (), s32[]{:S(2)}) async-start(), calls=%async_computation.6 | async-start | bytes 10485760 | tf_op jit(solution)/shard_map/all_gather | solution.py:67
  28.3 99.8 %copy-start = (bf16[32,8,16,128]{3,2,1,0:T(8,128)(2,1)}, bf16[32,8,16,128]{3,2,1,0:T(8,128)(2,1)S(1)}, u32[]{:S(2)}) copy-start(bf16[32,8,16,128]{3,2,1,0:T(8,128)(2,1)S(1)} %copy.77) | copy-start | bytes 3145732
  29.1 1.3 copy-start.11
  128.1 148.3 %copy-start.13 = (f32[2048]{0:T(1024)S(1)}, f32[2048]{0:T(1024)}, u32[]{:S(2)}) copy-start(f32[2048]{0:T(1024)} %param.13) | copy-start | bytes 24580
  276.4 12.6 %copy-start.10 = (f32[256,16,128]{0,2,1:T(8,128)S(1)}, f32[256,16,128]{0,2,1:T(8,128)}, u32[]{:S(2)}) copy-start(f32[256,16,128]{0,2,1:T(8,128)} %get-tuple-element.128) | copy-start | bytes 6291460
  293.0 15.8 %all-to-all-start.1 = ((bf16[256,4,512]{2,0,1:T(8,128)(2,1)}), bf16[256,4,512]{2,0,1:T(8,128)(2,1)}, u32[]{:S(2)}, u32[]{:S(2)}) async-start(bf16[256,4,512]{2,0,1:T(8,128)(2,1)} %copy.69), calls=%async_computation.1 | async-start | bytes 2097152 | tf_op jit(solution)/shard_map/all_to_all | solution.py:61
  297.2 107.9 %reduce-scatter.2.cloned.1.call-start = ((), (), s32[]{:S(2)}) async-start(), calls=%async_computation.3 | async-start | bytes 4325376 | tf_op jit(solution)/shard_map/reduce_scatter | solution.py:72
  319.1 201.1 %all-gather.9.cloned.1.call-start = ((), (), s32[]{:S(2)}) async-start(), calls=%async_computation.5 | async-start | bytes 34603008 | tf_op jit(solution)/shard_map/all_gather | solution.py:16
  324.4 1.2 copy-start.4
  325.6 1.4 copy-start.8
  331.4 3.5 copy-start.2
  567.5 1.2 copy-start.1
  567.5 1.9 copy-start.9
  570.0 1.4 copy-start.7
Sparse Core Ops, SparseCore 0:
  11.6 116.3 all-gather.6
  129.6 147.7 all-gather.10
  319.3 85.7 reduce-scatter.1
  407.2 113.0 all-gather.8
